TPU v7x, 512 devices: a whole 4x8x8 slice. The times are simulated.
512 devices in a mesh: dp: 32 (over x, y), expert: 16 (over z, core).
Axes of the slice: x: 4, y: 8, z: 8, core: 2. Of those that a mesh axis runs over, the one named last changes fastest.
Arguments:
- tokens: bfloat16 [8192, 2048], P('expert', 'dp'), may hold values from -6 to 6
- routes: int32 [8192, 2], P('expert'), may hold values from 0 to 15, all different within a row; in each aligned block of 512 rows (0 to 511, 512 to 1023, ...) at most 96 rows name the same one
- scores: int32 [8192, 2], P('expert'), may hold values from 1 to 1023
- gate_weight: bfloat16 [16, 2048, 8192], P('expert', None, 'dp'), may hold values from -0.125 to 0.125
- up_weight: bfloat16 [16, 2048, 8192], P('expert', None, 'dp'), may hold values from -0.125 to 0.125
- down_weight: bfloat16 [16, 8192, 2048], P('expert', 'dp'), may hold values from -0.0625 to 0.0625
Outputs:
- layer_out: bfloat16 [8192, 2048], P('expert', 'dp')
Inputs may be any that keep to these rules, and one draw needn't show every extreme that they name: `routes`: each row names 2 different experts. Within each aligned block of 512 rows no expert is named by more than 96 rows, and in every draw some expert is named by exactly 96 rows of a block.
All inputs are finite; a program needn't handle non-finite values.
Results may differ from a plain program's by a relative error of at most 0.025.
Values may be sent and summed in bfloat16 or wider, within the bound.
A program may use at most 64 MiB of HBM per device.

v0:
```python
import jax
import jax.numpy as jnp
from jax import lax
from jax.sharding import PartitionSpec as P


def shards(tokens, routes, scores, gate_weight, up_weight, down_weight):
    expert_count = lax.axis_size("expert")
    row_count = tokens.shape[0]
    local_cols = tokens.shape[1]
    capacity = 3 * row_count // expert_count
    slot_count = expert_count * capacity
    expert_ids = jnp.arange(expert_count, dtype=jnp.int32)
    onehot = (routes[:, :, None] == expert_ids[None, None, :]).astype(jnp.int32)
    named = jnp.sum(onehot, axis=1)
    earlier = jnp.cumsum(named, axis=0) - named
    slot_rank = jnp.sum(onehot * earlier[:, None, :], axis=2)
    target = routes * capacity + slot_rank
    slot_ids = jnp.arange(slot_count, dtype=jnp.int32)
    placement = jnp.any(target[None, :, :] == slot_ids[:, None, None], axis=2).astype(jnp.bfloat16)
    weight = scores.astype(jnp.float32)
    weight = weight / jnp.sum(weight, axis=1, keepdims=True)
    gate_mat = gate_weight[0]
    up_mat = up_weight[0]
    down_mat = down_weight[0]
    outgoing = jnp.dot(placement, tokens, preferred_element_type=jnp.float32).astype(jnp.bfloat16)
    arrived = lax.all_to_all(
        outgoing.reshape(expert_count, capacity, local_cols),
        "expert",
        split_axis=0,
        concat_axis=0,
        tiled=True,
    )
    arrived = arrived.reshape(slot_count, local_cols)
    piece = lax.all_gather(arrived, "dp", axis=1, tiled=True)
    gate = jnp.dot(piece, gate_mat, preferred_element_type=jnp.float32)
    upval = jnp.dot(piece, up_mat, preferred_element_type=jnp.float32)
    hidden = (jax.nn.silu(gate) * upval).astype(jnp.bfloat16)
    summed = lax.psum_scatter(
        lax.dot_general(
            down_mat, hidden, (((0,), (1,)), ((), ())), preferred_element_type=jnp.float32
        ).astype(jnp.bfloat16),
        "dp",
        scatter_dimension=0,
        tiled=True,
    ).astype(jnp.float32)
    returned = lax.all_to_all(
        summed.reshape(local_cols, expert_count, capacity).astype(jnp.bfloat16),
        "expert",
        split_axis=1,
        concat_axis=1,
        tiled=True,
    ).astype(jnp.float32)
    returned = returned.reshape(local_cols, slot_count)
    first_part = jnp.take(returned, target[:, 0], axis=1)
    second_part = jnp.take(returned, target[:, 1], axis=1)
    combined = (first_part * weight[:, 0][None, :] + second_part * weight[:, 1][None, :]).T
    return combined.astype(jnp.bfloat16)


def solution(mesh):
    return jax.shard_map(
        shards,
        mesh=mesh,
        in_specs=(
            P("expert", "dp"),
            P("expert", None),
            P("expert", None),
            P("expert", None, "dp"),
            P("expert", None, "dp"),
            P("expert", "dp", None),
        ),
        out_specs=P("expert", "dp"),
        check_vma=False,
    )
```

profile of v0, /device:TPU:1, one launch (start us, length us, event | category | flops | bytes accessed | tf_op | source)
XLA Modules:
  0.0 414.6 jit_solution(14097522096676943779)
XLA Ops:
  6.5 0.8 convert_reduce_fusion
  7.3 1.2 reduce-window.6
  8.5 0.2 slice_reduce_fusion
  8.8 0.7 select_reduce_fusion
  9.6 0.7 multiply_add_fusion
  10.3 2.0 fusion.1
  12.2 1.4 convolution_convert_fusion.1
  13.7 0.2 reshape.37
  14.0 23.3 %all_to_all.10 = bf16[16,96,64]{1,2,0:T(8,128)(2,1)S(1)} all-to-all(bf16[16,96,64]{1,2,0:T(8,128)(2,1)S(1)} %copy.37), channel_id=1, replica_groups=mesh['dp'=32,'expert'=16] {'expert'}, dimensions={0} | all-to-all | bytes 393216 | tf_op jit(solution)/shard_map/all_to_all | solution.py:27
  37.5 0.9 reshape.38
  38.5 89.9 %all-gather.2.cloned.1.call-done = bf16[1536,2048]{0,1:T(8,128)(2,1)} async-done(((bf16[1536,64]{0,1:T(8,128)(2,1)}), bf16[1536,2048]{0,1:T(8,128)(2,1)}) %all-gather.2.cloned.1.call-update) | async-done | bytes 6291472 | tf_op jit(solution)/shard_map/all_gather | solution.py:35
  128.4 6.1 %fusion.6 = f32[1536,256]{1,0:T(8,128)} fusion(bf16[1536,2048]{0,1:T(8,128)(2,1)} %all-gather.2.cloned.1.call-done, bf16[1,2048,256]{2,1,0:T(8,128)(2,1)} %param.11), kind=kOutput, calls=%fused_computation.11 | convolution fusion | flops 1610612736 | bytes 8912896 | tf_op jit(solution)/shard_map/dot_general | solution.py:36
  134.5 12.3 %fusion = bf16[2048,1536]{0,1:T(8,128)(2,1)} fusion(bf16[1536,2048]{0,1:T(8,128)(2,1)} %all-gather.2.cloned.1.call-done, f32[1536,256]{1,0:T(8,128)} %fusion.6, bf16[1,256,2048]{2,1,0:T(8,128)(2,1)S(1)} %copy-done, bf16[1,2048,256]{2,1,0:T(8,128)(2,1)S(1)} %copy-done.2), kind=kOutput, calls=%fused_computation.3 | convolution fusion | flops 3226730496 | bytes 16252928 | tf_op jit(solution)/shard_map/dot_general | solution.py:40
  146.8 8.7 %copy.42 = bf16[2048,1536]{1,0:T(8,128)(2,1)} copy(bf16[2048,1536]{0,1:T(8,128)(2,1)} %fusion) | data formatting | bytes 12582912
  155.5 0.7 copy-done.1
  156.3 222.8 %reduce-scatter.4.cloned.1.call-done = bf16[64,1536]{1,0:T(8,128)(2,1)} async-done(((bf16[2048,1536]{1,0:T(8,128)(2,1)}), bf16[64,1536]{1,0:T(8,128)(2,1)}) %reduce-scatter.4.cloned.1.call-update) | async-done | bytes 196624
  379.0 1.1 copy.43
  380.2 0.9 copy.39
  381.0 11.6 %all-to-all-start.1 = ((bf16[64,16,96]{2,0,1:T(8,128)(2,1)}), bf16[64,16,96]{2,0,1:T(8,128)(2,1)S(1)}, u32[]{:S(2)}, u32[]{:S(2)}) async-start(bf16[64,16,96]{2,0,1:T(8,128)(2,1)} %copy.39), calls=%async_computation.1 | async-start | bytes 524288 | tf_op jit(solution)/shard_map/all_to_all | solution.py:47
  392.7 11.7 %all-to-all-done.1 = bf16[64,16,96]{2,0,1:T(8,128)(2,1)S(1)} async-done(((bf16[64,16,96]{2,0,1:T(8,128)(2,1)}), bf16[64,16,96]{2,0,1:T(8,128)(2,1)S(1)}, u32[]{:S(2)}, u32[]{:S(2)}) %all-to-all-start.1) | async-done | bytes 196640 | tf_op jit(solution)/shard_map/all_to_all | solution.py:47
  404.6 1.0 gather_fusion
  405.6 1.0 gather_fusion.1
  406.6 0.3 fusion.11
  407.0 0.7 copy.41
  (25 shorter events, 0.7 us)
Async XLA Ops:
  6.5 128.0 %copy-start = (bf16[1,256,2048]{2,1,0:T(8,128)(2,1)S(1)}, bf16[1,256,2048]{2,1,0:T(8,128)(2,1)}, u32[]{:S(2)}) copy-start(bf16[1,256,2048]{2,1,0:T(8,128)(2,1)} %param.13) | copy-start | bytes 3145732
  6.5 121.9 %all-gather.2.cloned.1.call-start = ((), (), s32[]{:S(2)}) async-start(), calls=%async_computation.3 | async-start | bytes 6488064 | tf_op jit(solution)/shard_map/all_gather | solution.py:35
  38.5 96.0 %copy-start.2 = (bf16[1,2048,256]{2,1,0:T(8,128)(2,1)S(1)}, bf16[1,2048,256]{2,1,0:T(8,128)(2,1)}, u32[]{:S(2)}) copy-start(bf16[1,2048,256]{2,1,0:T(8,128)(2,1)} %param.12) | copy-start | bytes 3145732
  38.5 340.5 %reduce-scatter.4.cloned.1.call-start = ((), (), s32[]{:S(2)}) async-start(), calls=%async_computation.4 | async-start | bytes 6488064
  155.5 0.7 copy-start.1
  381.0 23.3 %all-to-all-start.1 = ((bf16[64,16,96]{2,0,1:T(8,128)(2,1)}), bf16[64,16,96]{2,0,1:T(8,128)(2,1)S(1)}, u32[]{:S(2)}, u32[]{:S(2)}) async-start(bf16[64,16,96]{2,0,1:T(8,128)(2,1)} %copy.39), calls=%async_computation.1 | async-start | bytes 524288 | tf_op jit(solution)/shard_map/all_to_all | solution.py:47
Sparse Core Ops, SparseCore 0:
  38.6 89.7 all-gather.1
  155.6 223.3 reduce-scatter.3
where the time goes:
time: 415 us
  waiting for transfers between devices  324 us (78%)
  blocking collectives  23.3 us (6%)
  matrix products  19.8 us (5%)
  local copies, waits for them, and re-layouts  16 us (4%)
  between operations  13.5 us (3%)
  starting transfers between devices  11.7 us (3%)
  other arithmetic  5.85 us (1%)
    unnamed x3, waiting for transfers between devices  223 us
    all_gather x1, waiting for transfers between devices, shards(): piece = lax.all_gather(arrived, 'dp', axis=1, tiled=True)  89.9 us
    all_to_all x1, blocking collectives, shards(): lax.all_to_all(outgoing.reshape(expert_count, capacity, local_cols), 'exp...  23.3 us
    dot_general x1, matrix products, shards(): lax.dot_general(down_mat, hidden, (((0,), (1,)), ((), ())), preferred_ele...  12.3 us
    all_to_all x1, waiting for transfers between devices, shards(): lax.all_to_all(summed.reshape(local_cols, expert_count, capacity).astype(...  11.7 us
    all_to_all x1, starting transfers between devices, shards(): lax.all_to_all(summed.reshape(local_cols, expert_count, capacity).astype(...  11.6 us
    unnamed x8, local copies, waits for them, and re-layouts  10.5 us
  transfers between devices with their start and end apart: 3, of which 3 were waited for; matrix products, arithmetic and copies ran while one was open for 0% of the time, Pallas kernels for 0%

commit v1 on v0

--- a/solution.py
+++ b/solution.py
@@ -2,6 +2,13 @@
 import jax.numpy as jnp
 from jax import lax
 from jax.sharding import PartitionSpec as P
+
+
+def swap_blocks(shard, axis, split, join):
+    size = lax.axis_size(axis)
+    shards = jnp.stack(jnp.split(shard, size, axis=split), axis=0)
+    shards = lax.all_to_all(shards, axis, split_axis=0, concat_axis=0)
+    return jnp.concatenate(shards, axis=join)
 
 
 def shards(tokens, routes, scores, gate_weight, up_weight, down_weight):
@@ -44,12 +51,8 @@
         scatter_dimension=0,
         tiled=True,
     ).astype(jnp.float32)
-    returned = lax.all_to_all(
-        summed.reshape(local_cols, expert_count, capacity).astype(jnp.bfloat16),
-        "expert",
-        split_axis=1,
-        concat_axis=1,
-        tiled=True,
+    returned = swap_blocks(
+        summed.reshape(local_cols, expert_count, capacity).astype(jnp.bfloat16), "expert", 1, 1
     ).astype(jnp.float32)
     returned = returned.reshape(local_cols, slot_count)
     first_part = jnp.take(returned, target[:, 0], axis=1)

time: 415 us -> 426 us (1.027)
  local copies, waits for them, and re-layouts: 16 us -> 26.4 us
    unnamed x8 -> x39, local copies, waits for them, and re-layouts: 10.5 us -> 21 us
where the time goes in v1:
time: 426 us; the launch traced here: 425 us
  waiting for transfers between devices  324 us (76%)
  local copies, waits for them, and re-layouts  26.4 us (6%)
  blocking collectives  23.3 us (5%)
  matrix products  19.9 us (5%)
  between operations  13.7 us (3%)
  starting transfers between devices  11.8 us (3%)
  other arithmetic  5.89 us (1%)
    unnamed x3, waiting for transfers between devices  223 us
    all_gather x1, waiting for transfers between devices, shards(): piece = lax.all_gather(arrived, 'dp', axis=1, tiled=True)  89.7 us
    all_to_all x1, blocking collectives, shards(): lax.all_to_all(outgoing.reshape(expert_count, capacity, local_cols), 'exp...  23.3 us
    unnamed x39, local copies, waits for them, and re-layouts  21 us
    dot_general x1, matrix products, shards(): lax.dot_general(down_mat, hidden, (((0,), (1,)), ((), ())), preferred_ele...  12.3 us
    all_to_all x1, waiting for transfers between devices, swap_blocks(): shards = lax.all_to_all(shards, axis, split_axis=0, concat_axis=0)  11.7 us
    all_to_all x1, starting transfers between devices, swap_blocks(): shards = lax.all_to_all(shards, axis, split_axis=0, concat_axis=0)  11.6 us
  transfers between devices with their start and end apart: 3, of which 3 were waited for; matrix products, arithmetic and copies ran while one was open for 0% of the time, Pallas kernels for 0%

profile of v1, /device:TPU:1, one launch (start us, length us, event | category | flops | bytes accessed | tf_op | source)
XLA Modules:
  0.0 425.2 jit_solution(3388124802342850777)
XLA Ops:
  6.5 0.8 convert_reduce_fusion
  7.3 1.2 reduce-window.6
  8.8 0.7 select_reduce_fusion
  9.6 0.7 multiply_add_fusion
  10.3 2.0 fusion.1
  12.2 1.4 convolution_convert_fusion.1
  14.0 23.3 %all_to_all.10 = bf16[16,96,64]{1,2,0:T(8,128)(2,1)S(1)} all-to-all(bf16[16,96,64]{1,2,0:T(8,128)(2,1)S(1)} %copy.67), channel_id=1, replica_groups=mesh['dp'=32,'expert'=16] {'expert'}, dimensions={0} | all-to-all | bytes 393216 | tf_op jit(solution)/shard_map/all_to_all | solution.py:34
  37.5 0.9 reshape.38
  38.7 89.7 %all-gather.2.cloned.1.call-done = bf16[1536,2048]{0,1:T(8,128)(2,1)} async-done(((bf16[1536,64]{0,1:T(8,128)(2,1)}), bf16[1536,2048]{0,1:T(8,128)(2,1)}) %all-gather.2.cloned.1.call-update) | async-done | bytes 6291472 | tf_op jit(solution)/shard_map/all_gather | solution.py:42
  128.4 6.1 %fusion.6 = f32[1536,256]{1,0:T(8,128)} fusion(bf16[1536,2048]{0,1:T(8,128)(2,1)} %all-gather.2.cloned.1.call-done, bf16[1,2048,256]{2,1,0:T(8,128)(2,1)} %param.11), kind=kOutput, calls=%fused_computation.11 | convolution fusion | flops 1610612736 | bytes 8912896 | tf_op jit(solution)/shard_map/dot_general | solution.py:43
  134.5 12.3 %fusion = bf16[2048,1536]{0,1:T(8,128)(2,1)} fusion(bf16[1536,2048]{0,1:T(8,128)(2,1)} %all-gather.2.cloned.1.call-done, f32[1536,256]{1,0:T(8,128)} %fusion.6, bf16[1,256,2048]{2,1,0:T(8,128)(2,1)S(1)} %copy-done, bf16[1,2048,256]{2,1,0:T(8,128)(2,1)S(1)} %copy-done.2), kind=kOutput, calls=%fused_computation.3 | convolution fusion | flops 3226730496 | bytes 16252928 | tf_op jit(solution)/shard_map/dot_general | solution.py:47
  146.8 8.7 %copy.87 = bf16[2048,1536]{1,0:T(8,128)(2,1)} copy(bf16[2048,1536]{0,1:T(8,128)(2,1)} %fusion) | data formatting | bytes 12582912
  155.5 0.7 copy-done.1
  156.2 222.9 %reduce-scatter.4.cloned.1.call-done = bf16[64,1536]{1,0:T(8,128)(2,1)} async-done(((bf16[2048,1536]{1,0:T(8,128)(2,1)}), bf16[64,1536]{1,0:T(8,128)(2,1)}) %reduce-scatter.4.cloned.1.call-update) | async-done | bytes 196624
  379.1 1.2 copy.88
  380.4 0.6 constant_dynamic-update-slice_fusion.15
  382.6 0.6 constant_dynamic-update-slice_fusion.14
  388.6 0.6 constant_dynamic-update-slice_fusion.4
  390.4 0.6 constant_dynamic-update-slice_fusion.1
  391.6 11.6 %all-to-all-start.1 = ((bf16[16,64,1,96]{3,1,2,0:T(8,128)(2,1)}), bf16[16,64,1,96]{3,1,2,0:T(8,128)(2,1)S(1)}, u32[]{:S(2)}, u32[]{:S(2)}) async-start(bf16[16,64,1,96]{3,1,2,0:T(8,128)(2,1)} %constant_dynamic-update-slice_fusion), calls=%async_computation.1 | async-start | bytes 524288 | tf_op jit(solution)/shard_map/all_to_all | solution.py:10
  403.2 11.7 %all-to-all-done.1 = bf16[16,64,1,96]{3,1,2,0:T(8,128)(2,1)S(1)} async-done(((bf16[16,64,1,96]{3,1,2,0:T(8,128)(2,1)}), bf16[16,64,1,96]{3,1,2,0:T(8,128)(2,1)S(1)}, u32[]{:S(2)}, u32[]{:S(2)}) %all-to-all-start.1) | async-done | bytes 196640 | tf_op jit(solution)/shard_map/all_to_all | solution.py:10
  415.2 1.0 gather_fusion
  416.3 1.0 gather_fusion.1
  417.6 0.7 copy.86
  (57 shorter events, 10.5 us)
Async XLA Ops:
  6.5 128.0 %copy-start = (bf16[1,256,2048]{2,1,0:T(8,128)(2,1)S(1)}, bf16[1,256,2048]{2,1,0:T(8,128)(2,1)}, u32[]{:S(2)}) copy-start(bf16[1,256,2048]{2,1,0:T(8,128)(2,1)} %param.13) | copy-start | bytes 3145732
  6.5 121.9 %all-gather.2.cloned.1.call-start = ((), (), s32[]{:S(2)}) async-start(), calls=%async_computation.3 | async-start | bytes 6488064 | tf_op jit(solution)/shard_map/all_gather | solution.py:42
  38.5 96.0 %copy-start.2 = (bf16[1,2048,256]{2,1,0:T(8,128)(2,1)S(1)}, bf16[1,2048,256]{2,1,0:T(8,128)(2,1)}, u32[]{:S(2)}) copy-start(bf16[1,2048,256]{2,1,0:T(8,128)(2,1)} %param.12) | copy-start | bytes 3145732
  38.5 340.6 %reduce-scatter.4.cloned.1.call-start = ((), (), s32[]{:S(2)}) async-start(), calls=%async_computation.4 | async-start | bytes 6488064
  155.5 0.7 copy-start.1
  391.6 23.3 %all-to-all-start.1 = ((bf16[16,64,1,96]{3,1,2,0:T(8,128)(2,1)}), bf16[16,64,1,96]{3,1,2,0:T(8,128)(2,1)S(1)}, u32[]{:S(2)}, u32[]{:S(2)}) async-start(bf16[16,64,1,96]{3,1,2,0:T(8,128)(2,1)} %constant_dynamic-update-slice_fusion), calls=%async_computation.1 | async-start | bytes 524288 | tf_op jit(solution)/shard_map/all_to_all | solution.py:10
Sparse Core Ops, SparseCore 0:
  38.6 89.7 all-gather.1
  155.6 223.4 reduce-scatter.3
